TPU v7x, 32 devices: a whole 2x2x4 slice. The times are simulated.
32 devices in a mesh: dp: 2 (over y), tm: 8 (over z, core), height: 2 (over x).
Axes of the slice: x: 2, y: 2, z: 4, core: 2. Of those that a mesh axis runs over, the one named last changes fastest.
Arguments:
- clip_input: bfloat16 [2, 32, 8, 96, 128], P('dp', 'tm', 'height'), may hold values from -6 to 6
- cotangent: bfloat16 [2, 32, 8, 96, 128], P('dp', 'tm', 'height'), may hold values from -6 to 6
- first_kernel: bfloat16 [2592, 96], replicated, may hold values from -0.125 to 0.125
- second_kernel: bfloat16 [2592, 96], replicated, may hold values from -0.125 to 0.125
Outputs:
- block_output: float32 [2, 32, 8, 96, 128], P('dp', 'tm', 'height')
- input_grad: float32 [2, 32, 8, 96, 128], P('dp', 'tm', 'height')
- first_grad: float32 [2592, 96], P('dp')
- second_grad: float32 [2592, 96], P('dp')
All inputs are finite; a program needn't handle non-finite values.
Results may differ from a plain program's by a relative error of at most 0.0048.
Values may be sent and summed in bfloat16 or wider, within the bound.
A program may use at most 64 MiB of HBM per device.

v0:
```python
import math
import jax
import jax.numpy as jnp
from jax import lax
from jax.sharding import PartitionSpec as P

EPSILON = 1e-06


def extended_2(array, sides, width):
    for axis, dim in sides:
        peers, length = (lax.axis_size(axis), array.shape[dim])
        up = [(i, (i + 1) % peers) for i in range(peers - 1)]
        down = [(j, i) for i, j in up]
        last = lax.slice_in_dim(array, length - width, length, axis=dim)
        first = lax.slice_in_dim(array, 0, width, axis=dim)
        before = lax.ppermute(last, axis, up)
        after = lax.ppermute(first, axis, down)
        array = jnp.concatenate([before, array, after], axis=dim)
    return array


def passed_along(array, axis, by):
    peers = lax.axis_size(axis)
    pairs = [(i, i + by) for i in range(peers) if 0 <= i + by < peers]
    return lax.ppermute(array, axis, pairs)


def norm_silu(field):
    factor = lax.rsqrt(jnp.mean(field * field, axis=2, keepdims=True) + EPSILON)
    return jax.nn.silu(field * factor)


def pad_rows(extended):
    rimmed = extended_2(extended, (("height", 1),), 1)
    return jnp.pad(rimmed, ((0, 0), (0, 0), (0, 0), (1, 1)))


def time_stack(padded, tap_row, tap_col, frames):
    row_count = padded.shape[1] - 2
    col_count = padded.shape[3] - 2
    window = padded[:, tap_row : tap_row + row_count, :, tap_col : tap_col + col_count]
    return jnp.concatenate([window[offset : offset + frames] for offset in range(3)], axis=2)


def local_conv(padded, kernel, frames):
    channels = padded.shape[2]
    summed = None
    for tap_row in range(3):
        for tap_col in range(3):
            stacked = time_stack(padded, tap_row, tap_col, frames)
            weight = kernel[:, tap_row, tap_col].reshape(3 * channels, kernel.shape[4])
            partial_sum = jnp.einsum(
                "frkw,kd->frdw", stacked, weight, preferred_element_type=jnp.float32
            )
            summed = partial_sum if summed is None else summed + partial_sum
    return summed


def kernel_grad(padded, grad_out, frames):
    channels = padded.shape[2]
    row_list = []
    for tap_row in range(3):
        col_list = []
        for tap_col in range(3):
            stacked = time_stack(padded, tap_row, tap_col, frames)
            piece = jnp.einsum(
                "frkw,frdw->kd", stacked, grad_out, preferred_element_type=jnp.float32
            )
            col_list.append(piece.reshape(3, channels, grad_out.shape[2]))
        row_list.append(jnp.stack(col_list, axis=1))
    gathered = jnp.stack(row_list, axis=1)
    return gathered.reshape(27 * channels, grad_out.shape[2])


def flipped(kernel):
    return jnp.swapaxes(kernel[::-1, ::-1, ::-1], 3, 4)


def local(clip_input, cotangent, first_kernel, second_kernel):
    frames = clip_input.shape[1]
    channels = clip_input.shape[3]
    source = clip_input[0]
    upstream = cotangent[0]
    kernel_one = first_kernel.reshape(3, 3, 3, channels, channels)
    kernel_two = second_kernel.reshape(3, 3, 3, channels, channels)

    def extend_back(block):
        earlier = passed_along(block[frames - 2 :], "tm", 1)
        return pad_rows(jnp.concatenate([earlier, block], axis=0))

    def extend_ahead(block):
        later = passed_along(block[:2], "tm", -1)
        return pad_rows(jnp.concatenate([block, later], axis=0))

    source_float = source.astype(jnp.float32)
    first_act = norm_silu(source_float).astype(jnp.bfloat16)
    first_padded = extend_back(first_act)
    middle = local_conv(first_padded, kernel_one, frames)
    second_act = norm_silu(middle).astype(jnp.bfloat16)
    second_padded = extend_back(second_act)
    branch = local_conv(second_padded, kernel_two, frames)
    block_output = source_float + branch
    second_back = local_conv(extend_ahead(upstream), flipped(kernel_two), frames)
    unused, pull_mid = jax.vjp(norm_silu, middle)
    middle_grad = pull_mid(second_back)[0].astype(jnp.bfloat16)
    first_back = local_conv(extend_ahead(middle_grad), flipped(kernel_one), frames)
    unused, pull_src = jax.vjp(norm_silu, source_float)
    input_grad = upstream.astype(jnp.float32) + pull_src(first_back)[0]
    positions = (
        frames
        * source.shape[1]
        * source.shape[3]
        * lax.axis_size("dp")
        * lax.axis_size("tm")
        * lax.axis_size("height")
    )
    factor = 1.0 / math.sqrt(positions)
    first_term = kernel_grad(first_padded, middle_grad, frames) * factor
    second_term = kernel_grad(second_padded, upstream, frames) * factor
    first_whole, second_whole = lax.psum((first_term, second_term), ("tm", "height"))
    first_grad, second_grad = (
        lax.psum_scatter(first_whole, "dp", scatter_dimension=0, tiled=True),
        lax.psum_scatter(second_whole, "dp", scatter_dimension=0, tiled=True),
    )
    return (block_output[None], input_grad[None], first_grad, second_grad)


def solution(mesh):
    return jax.shard_map(
        local,
        mesh=mesh,
        in_specs=(
            P("dp", "tm", "height", None, None),
            P("dp", "tm", "height", None, None),
            P(),
            P(),
        ),
        out_specs=(
            P("dp", "tm", "height", None, None),
            P("dp", "tm", "height", None, None),
            P("dp", None),
            P("dp", None),
        ),
        check_vma=False,
    )
```

profile of v0, /device:TPU:0, one launch (start us, length us, event | category | flops | bytes accessed | tf_op | source)
XLA Modules:
  0.0 240.6 jit_solution(6959624439068643985)
XLA Ops:
  8.2 1.3 collective-permute-start.6
  10.6 1.2 fusion.124
  11.9 3.2 %collective-permute-start = (bf16[2,4,96,128]{3,2,1,0:T(8,128)(2,1)S(1)}, bf16[2,4,96,128]{3,2,1,0:T(8,128)(2,1)S(1)}, u32[]{:S(2)}, u32[]{:S(2)}) collective-permute-start(bf16[2,4,96,128]{3,2,1,0:T(8,128)(2,1)S(1)} %slice.856), channel_id=1, source_target_pairs={{0,2},{2,4},{4,6},{6,8},{8,10},{10,12},{12,14},{1,3},{3,5},{5,7},{... | collective-permute-start | bytes 589832 | tf_op jit(solution)/shard_map/ppermute | solution.py:26
  25.4 4.9 %collective-permute-start.7 = (bf16[6,1,96,128]{3,2,1,0:T(8,128)(2,1)S(1)}, bf16[6,1,96,128]{3,2,1,0:T(8,128)(2,1)S(1)}, u32[]{:S(2)}, u32[]{:S(2)}) collective-permute-start(bf16[6,1,96,128]{3,2,1,0:T(8,128)(2,1)S(1)} %get-tuple-element.150), channel_id=1, source_target_pairs={{0,1},{2,3},{4,5},{6,7},{8,9},{10,11},{12,13},{14,15},{16,17},{18,... | collective-permute-start | bytes 442376 | tf_op jit(solution)/shard_map/ppermute | solution.py:17
  30.3 1.3 collective-permute-start.8
  31.6 1.3 collective-permute-start.2
  32.9 4.6 %collective-permute-start.1 = (bf16[6,1,96,128]{3,2,1,0:T(8,128)(2,1)S(1)}, bf16[6,1,96,128]{3,2,1,0:T(8,128)(2,1)S(1)}, u32[]{:S(2)}, u32[]{:S(2)}) collective-permute-start(bf16[6,1,96,128]{3,2,1,0:T(8,128)(2,1)S(1)} %get-tuple-element.159), channel_id=1, source_target_pairs={{0,1},{2,3},{4,5},{6,7},{8,9},{10,11},{12,13},{14,15},{16,17},{18,... | collective-permute-start | bytes 442376 | tf_op jit(solution)/shard_map/ppermute | solution.py:17
  37.6 1.3 collective-permute-done.8
  39.9 2.0 fusion.211
  43.0 2.1 fusion.213
  62.3 1.3 collective-permute-start.9
  63.6 3.0 %collective-permute-start.3 = (bf16[2,4,96,128]{3,2,1,0:T(8,128)(2,1)S(1)}, bf16[2,4,96,128]{3,2,1,0:T(8,128)(2,1)S(1)}, u32[]{:S(2)}, u32[]{:S(2)}) collective-permute-start(bf16[2,4,96,128]{3,2,1,0:T(8,128)(2,1)S(1)} %slice.896), channel_id=1, source_target_pairs={{0,2},{2,4},{4,6},{6,8},{8,10},{10,12},{12,14},{1,3},{3,5},{5,7},{... | collective-permute-start | bytes 589832 | tf_op jit(solution)/shard_map/ppermute | solution.py:26
  68.7 1.3 collective-permute-start.5
  70.0 4.6 %collective-permute-start.4 = (bf16[6,1,96,128]{3,2,1,0:T(8,128)(2,1)S(1)}, bf16[6,1,96,128]{3,2,1,0:T(8,128)(2,1)S(1)}, u32[]{:S(2)}, u32[]{:S(2)}) collective-permute-start(bf16[6,1,96,128]{3,2,1,0:T(8,128)(2,1)S(1)} %get-tuple-element.155), channel_id=1, source_target_pairs={{0,1},{2,3},{4,5},{6,7},{8,9},{10,11},{12,13},{14,15},{16,17},{18,... | collective-permute-start | bytes 442376 | tf_op jit(solution)/shard_map/ppermute | solution.py:17
  74.7 1.3 collective-permute-start.10
  76.0 1.5 collective-permute-start.11
  81.9 2.0 fusion.212
  95.5 1.3 fusion.16
  100.0 3.1 %fusion.210 = (bf16[4,4,96,128]{3,2,1,0:T(8,128)(2,1)S(1)}, bf16[4,4,96,128]{3,2,1,0:T(8,128)(2,1)S(1)}, bf16[4,4,96,128]{3,2,1,0:T(8,128)(2,1)S(1)}, bf16[4,4,9...) fusion(bf16[6,6,96,130]{3,2,1,0:T(8,128)(2,1)S(1)} %select_maxi, ...), kind=kLoop, calls=%fused_computation.330 | loop fusion | bytes 14155776 | tf_op jit(solution)/shard_map/slice | solution.py:43
  103.5 1.8 fusion.78
  113.9 17.9 %reduce-scatter.5.cloned.1.call-done = f32[1296,96]{1,0:T(8,128)} async-done(((f32[2592,96]{1,0:T(8,128)}), f32[1296,96]{1,0:T(8,128)}) %reduce-scatter.5.cloned.1.call-update) | async-done | bytes 497680 | tf_op jit(solution)/shard_map/reduce_scatter | solution.py:124
  132.9 96.8 %all-reduce.7.cloned.1.call-done = (f32[1296,96]{1,0:T(8,128)}, f32[1296,96]{1,0:T(8,128)}) async-done(((f32[1296,96]{1,0:T(8,128)}, f32[1296,96]{1,0:T(8,128)}), (f32[1296,96]{1,0:T(8,128)}, f32[1296,96]{1,0:T(8,128)})) %all-reduce.7.cloned.1.call-update) | async-done | bytes 995344 | tf_op jit(solution)/shard_map/psum | solution.py:121
  229.8 2.1 copy.104
  231.9 2.1 copy.105
  (242 shorter events, 62.3 us)
Async XLA Ops:
  7.2 7.9 %copy-start.2 = (bf16[2592,96]{0,1:T(8,128)(2,1)S(1)}, bf16[2592,96]{0,1:T(8,128)(2,1)}, u32[]{:S(2)}) copy-start(bf16[2592,96]{0,1:T(8,128)(2,1)} %param.6) | copy-start | bytes 1492996
  7.2 106.7 %reduce-scatter.3.cloned.1.call-start = ((), (), s32[]{:S(2)}) async-start(), calls=%async_computation.2 | async-start | bytes 1990656 | tf_op jit(solution)/shard_map/reduce_scatter | solution.py:123
  8.2 17.1 %collective-permute-start.6 = (bf16[2,4,96,128]{3,2,1,0:T(8,128)(2,1)S(1)}, bf16[2,4,96,128]{3,2,1,0:T(8,128)(2,1)S(1)}, u32[]{:S(2)}, u32[]{:S(2)}) collective-permute-start(bf16[2,4,96,128]{3,2,1,0:T(8,128)(2,1)S(1)} %slice_bitcast_fusion), channel_id=1, source_target_pairs={{2,0},{4,2},{6,4},{8,6},{10,8},{12,10},{14,12},{3,1},{5,3},{7,5},{... | collective-permute-start | bytes 589832 | tf_op jit(solution)/shard_map/ppermute | solution.py:26
  11.9 4.4 %copy-start.3 = (bf16[2592,96]{0,1:T(8,128)(2,1)S(1)}, bf16[2592,96]{0,1:T(8,128)(2,1)}, u32[]{:S(2)}) copy-start(bf16[2592,96]{0,1:T(8,128)(2,1)} %param.7) | copy-start | bytes 1492996
  11.9 19.7 %collective-permute-start = (bf16[2,4,96,128]{3,2,1,0:T(8,128)(2,1)S(1)}, bf16[2,4,96,128]{3,2,1,0:T(8,128)(2,1)S(1)}, u32[]{:S(2)}, u32[]{:S(2)}) collective-permute-start(bf16[2,4,96,128]{3,2,1,0:T(8,128)(2,1)S(1)} %slice.856), channel_id=1, source_target_pairs={{0,2},{2,4},{4,6},{6,8},{8,10},{10,12},{12,14},{1,3},{3,5},{5,7},{... | collective-permute-start | bytes 589832 | tf_op jit(solution)/shard_map/ppermute | solution.py:26
  17.6 7.8 %copy-start = (bf16[1,4,4,96,128]{4,3,2,1,0:T(8,128)(2,1)S(1)}, bf16[1,4,4,96,128]{4,3,2,1,0:T(8,128)(2,1)}, u32[]{:S(2)}) copy-start(bf16[1,4,4,96,128]{4,3,2,1,0:T(8,128)(2,1)} %param.5) | copy-start | bytes 1179652
  25.4 12.2 %collective-permute-start.7 = (bf16[6,1,96,128]{3,2,1,0:T(8,128)(2,1)S(1)}, bf16[6,1,96,128]{3,2,1,0:T(8,128)(2,1)S(1)}, u32[]{:S(2)}, u32[]{:S(2)}) collective-permute-start(bf16[6,1,96,128]{3,2,1,0:T(8,128)(2,1)S(1)} %get-tuple-element.150), channel_id=1, source_target_pairs={{0,1},{2,3},{4,5},{6,7},{8,9},{10,11},{12,13},{14,15},{16,17},{18,... | collective-permute-start | bytes 442376 | tf_op jit(solution)/shard_map/ppermute | solution.py:17
  30.3 8.6 %collective-permute-start.8 = (bf16[6,1,96,128]{3,2,1,0:T(8,128)(2,1)S(1)}, bf16[6,1,96,128]{3,2,1,0:T(8,128)(2,1)S(1)}, u32[]{:S(2)}, u32[]{:S(2)}) collective-permute-start(bf16[6,1,96,128]{3,2,1,0:T(8,128)(2,1)S(1)} %get-tuple-element.151), channel_id=1, source_target_pairs={{1,0},{3,2},{5,4},{7,6},{9,8},{11,10},{13,12},{15,14},{17,16},{19,... | collective-permute-start | bytes 442376 | tf_op jit(solution)/shard_map/ppermute | solution.py:18
  31.6 10.4 %collective-permute-start.2 = (bf16[6,1,96,128]{3,2,1,0:T(8,128)(2,1)S(1)}, bf16[6,1,96,128]{3,2,1,0:T(8,128)(2,1)S(1)}, u32[]{:S(2)}, u32[]{:S(2)}) collective-permute-start(bf16[6,1,96,128]{3,2,1,0:T(8,128)(2,1)S(1)} %get-tuple-element.158), channel_id=1, source_target_pairs={{1,0},{3,2},{5,4},{7,6},{9,8},{11,10},{13,12},{15,14},{17,16},{19,... | collective-permute-start | bytes 442376 | tf_op jit(solution)/shard_map/ppermute | solution.py:18
  32.9 9.1 %collective-permute-start.1 = (bf16[6,1,96,128]{3,2,1,0:T(8,128)(2,1)S(1)}, bf16[6,1,96,128]{3,2,1,0:T(8,128)(2,1)S(1)}, u32[]{:S(2)}, u32[]{:S(2)}) collective-permute-start(bf16[6,1,96,128]{3,2,1,0:T(8,128)(2,1)S(1)} %get-tuple-element.159), channel_id=1, source_target_pairs={{0,1},{2,3},{4,5},{6,7},{8,9},{10,11},{12,13},{14,15},{16,17},{18,... | collective-permute-start | bytes 442376 | tf_op jit(solution)/shard_map/ppermute | solution.py:17
  62.3 12.3 %collective-permute-start.9 = (bf16[2,4,96,128]{3,2,1,0:T(8,128)(2,1)S(1)}, bf16[2,4,96,128]{3,2,1,0:T(8,128)(2,1)S(1)}, u32[]{:S(2)}, u32[]{:S(2)}) collective-permute-start(bf16[2,4,96,128]{3,2,1,0:T(8,128)(2,1)S(1)} %slice.975), channel_id=1, source_target_pairs={{2,0},{4,2},{6,4},{8,6},{10,8},{12,10},{14,12},{3,1},{5,3},{7,5},{... | collective-permute-start | bytes 589832 | tf_op jit(solution)/shard_map/ppermute | solution.py:26
  63.6 5.1 %collective-permute-start.3 = (bf16[2,4,96,128]{3,2,1,0:T(8,128)(2,1)S(1)}, bf16[2,4,96,128]{3,2,1,0:T(8,128)(2,1)S(1)}, u32[]{:S(2)}, u32[]{:S(2)}) collective-permute-start(bf16[2,4,96,128]{3,2,1,0:T(8,128)(2,1)S(1)} %slice.896), channel_id=1, source_target_pairs={{0,2},{2,4},{4,6},{6,8},{8,10},{10,12},{12,14},{1,3},{3,5},{5,7},{... | collective-permute-start | bytes 589832 | tf_op jit(solution)/shard_map/ppermute | solution.py:26
  68.6 63.1 %reduce-scatter.5.cloned.1.call-start = ((), (), s32[]{:S(2)}) async-start(), calls=%async_computation.3 | async-start | bytes 1990656 | tf_op jit(solution)/shard_map/reduce_scatter | solution.py:124
  68.7 10.2 %collective-permute-start.5 = (bf16[6,1,96,128]{3,2,1,0:T(8,128)(2,1)S(1)}, bf16[6,1,96,128]{3,2,1,0:T(8,128)(2,1)S(1)}, u32[]{:S(2)}, u32[]{:S(2)}) collective-permute-start(bf16[6,1,96,128]{3,2,1,0:T(8,128)(2,1)S(1)} %get-tuple-element.154), channel_id=1, source_target_pairs={{1,0},{3,2},{5,4},{7,6},{9,8},{11,10},{13,12},{15,14},{17,16},{19,... | collective-permute-start | bytes 442376 | tf_op jit(solution)/shard_map/ppermute | solution.py:18
  70.0 8.9 %collective-permute-start.4 = (bf16[6,1,96,128]{3,2,1,0:T(8,128)(2,1)S(1)}, bf16[6,1,96,128]{3,2,1,0:T(8,128)(2,1)S(1)}, u32[]{:S(2)}, u32[]{:S(2)}) collective-permute-start(bf16[6,1,96,128]{3,2,1,0:T(8,128)(2,1)S(1)} %get-tuple-element.155), channel_id=1, source_target_pairs={{0,1},{2,3},{4,5},{6,7},{8,9},{10,11},{12,13},{14,15},{16,17},{18,... | collective-permute-start | bytes 442376 | tf_op jit(solution)/shard_map/ppermute | solution.py:17
  74.7 18.9 %collective-permute-start.10 = (bf16[6,1,96,128]{3,2,1,0:T(8,128)(2,1)S(1)}, bf16[6,1,96,128]{3,2,1,0:T(8,128)(2,1)S(1)}, u32[]{:S(2)}, u32[]{:S(2)}) collective-permute-start(bf16[6,1,96,128]{3,2,1,0:T(8,128)(2,1)S(1)} %get-tuple-element.146), channel_id=1, source_target_pairs={{0,1},{2,3},{4,5},{6,7},{8,9},{10,11},{12,13},{14,15},{16,17},{18,... | collective-permute-start | bytes 442376 | tf_op jit(solution)/shard_map/ppermute | solution.py:17
  76.0 17.7 %collective-permute-start.11 = (bf16[6,1,96,128]{3,2,1,0:T(8,128)(2,1)S(1)}, bf16[6,1,96,128]{3,2,1,0:T(8,128)(2,1)S(1)}, u32[]{:S(2)}, u32[]{:S(2)}) collective-permute-start(bf16[6,1,96,128]{3,2,1,0:T(8,128)(2,1)S(1)} %get-tuple-element.147), channel_id=1, source_target_pairs={{1,0},{3,2},{5,4},{7,6},{9,8},{11,10},{13,12},{15,14},{17,16},{19,... | collective-permute-start | bytes 442376 | tf_op jit(solution)/shard_map/ppermute | solution.py:18
  100.0 3.5 %copy-start.29 = (bf16[3,1,1,96,96]{4,3,0,2,1:T(8,128)(2,1)S(1)}, bf16[3,1,1,96,96]{4,3,0,2,1:T(8,128)(2,1)}, u32[]{:S(2)}) copy-start(bf16[3,1,1,96,96]{4,3,0,2,1:T(8,128)(2,1)} %copy.77) | copy-start | bytes 165892
  103.1 2.2 copy-start.27
  103.1 126.6 %all-reduce.7.cloned.1.call-start = ((), (), s32[]{:S(2)}) async-start(), calls=%async_computation.4 | async-start | bytes 2654208 | tf_op jit(solution)/shard_map/psum | solution.py:121
  103.4 1.9 copy-start.14
  103.5 1.9 copy-start.15
  103.5 1.9 copy-start.16
  107.8 1.2 copy-start.25
  (38 other events, 38.4 us)
Sparse Core Ops, SparseCore 0:
  68.8 24.7 reduce-scatter.2
  103.2 28.5 reduce-scatter.4
  135.4 94.3 all-reduce.6
where the time goes:
time: 242 us; the launch traced here: 241 us
  waiting for transfers between devices  116 us (48%)
  local copies, waits for them, and re-layouts  41.9 us (17%)
  starting transfers between devices  29.9 us (12%)
  matrix products  27.2 us (11%)
  between operations  15 us (6%)
  other arithmetic  10.3 us (4%)
    psum x1, waiting for transfers between devices, local(): lax.psum((first_term, second_term), ('tm', 'height'))  96.8 us
    dot_general x36, matrix products, local_conv(): jnp.einsum('frkw,kd->frdw', stacked, weight, preferred_element_type=jnp.f...  19 us
    reduce_scatter x1, waiting for transfers between devices, local(): lax.psum_scatter(second_whole, 'dp', scatter_dimension=0, tiled=True)  17.9 us
    unnamed x98, local copies, waits for them, and re-layouts  16.4 us
    ppermute x4, starting transfers between devices, extended_2(): before = lax.ppermute(last, axis, up)  15.3 us
    slice x10, local copies, waits for them, and re-layouts, time_stack(): window[offset:offset + frames]  12.6 us
    slice x22, local copies, waits for them, and re-layouts, local_conv(): weight = kernel[:, tap_row, tap_col].reshape(3 * channels, kernel.shape[4])  9.43 us
    ppermute x4, starting transfers between devices, passed_along(): return lax.ppermute(array, axis, pairs)  8.8 us
  transfers between devices with their start and end apart: 15, of which 4 were waited for; matrix products, arithmetic and copies ran while one was open for 19% of the time, Pallas kernels for 0%

commit v1 on v0

--- a/solution.py
+++ b/solution.py
@@ -118,7 +118,7 @@
     factor = 1.0 / math.sqrt(positions)
     first_term = kernel_grad(first_padded, middle_grad, frames) * factor
     second_term = kernel_grad(second_padded, upstream, frames) * factor
-    first_whole, second_whole = lax.psum((first_term, second_term), ("tm", "height"))
+    first_whole, second_whole = lax.psum(lax.psum((first_term, second_term), "height"), "tm")
     first_grad, second_grad = (
         lax.psum_scatter(first_whole, "dp", scatter_dimension=0, tiled=True),
         lax.psum_scatter(second_whole, "dp", scatter_dimension=0, tiled=True),

time: 242 us -> 253 us (1.045)
  waiting for transfers between devices: 116 us -> 123 us
  matrix products: 27.2 us -> 31.2 us
    psum x1 -> x2, waiting for transfers between devices: 96.8 us -> 104 us  [the longest x1 61.3 us: local(): lax.psum(lax.psum((first_term, second_term), 'height'), 'tm')]
    reduce_scatter x1, waiting for transfers between devices: 17.9 us -> 12.7 us  [local(): lax.psum_scatter(second_whole, 'dp', scatter_dimension=0, tiled=True)]
    dot_general x36, matrix products: 19 us -> 23 us  [local_conv(): jnp.einsum('frkw,kd->frdw', stacked, weight, preferred_element_type=jnp.f...]
    ppermute x4, waiting for transfers between devices: 1.46 us -> 4.33 us  [extended_2(): after = lax.ppermute(first, axis, down)]
    unnamed x98 -> x146, local copies, waits for them, and re-layouts: 16.4 us -> 16.1 us
  transfers between devices with their start and end apart: 15 -> 16, of which waited for: 4 -> 7; matrix products, arithmetic and copies ran while one was open for 19% -> 20% of each run, Pallas kernels for 0% -> 0%
where the time goes in v1:
time: 253 us; the launch traced here: 252 us
  waiting for transfers between devices  123 us (49%)
  local copies, waits for them, and re-layouts  42.2 us (17%)
  matrix products  31.2 us (12%)
  starting transfers between devices  29.9 us (12%)
  between operations  15.2 us (6%)
  other arithmetic  10.3 us (4%)
    psum x1, waiting for transfers between devices, local(): lax.psum(lax.psum((first_term, second_term), 'height'), 'tm')  61.3 us
    psum x1, waiting for transfers between devices, local(): lax.psum((first_term, second_term), 'height')  42.6 us
    dot_general x36, matrix products, local_conv(): jnp.einsum('frkw,kd->frdw', stacked, weight, preferred_element_type=jnp.f...  23 us
    unnamed x146, local copies, waits for them, and re-layouts  16.1 us
    ppermute x4, starting transfers between devices, extended_2(): before = lax.ppermute(last, axis, up)  15.3 us
    slice x10, local copies, waits for them, and re-layouts, time_stack(): window[offset:offset + frames]  13.2 us
    reduce_scatter x1, waiting for transfers between devices, local(): lax.psum_scatter(second_whole, 'dp', scatter_dimension=0, tiled=True)  12.7 us
    ppermute x4, starting transfers between devices, passed_along(): return lax.ppermute(array, axis, pairs)  8.79 us
  transfers between devices with their start and end apart: 16, of which 7 were waited for; matrix products, arithmetic and copies ran while one was open for 20% of the time, Pallas kernels for 0%

profile of v1, /device:TPU:0, one launch (start us, length us, event | category | flops | bytes accessed | tf_op | source)
XLA Modules:
  0.0 252.1 jit_solution(16791902247732622381)
XLA Ops:
  7.2 1.7 slice_bitcast_fusion
  12.5 3.2 %collective-permute-start = (bf16[2,4,96,128]{3,2,1,0:T(8,128)(2,1)S(1)}, bf16[2,4,96,128]{3,2,1,0:T(8,128)(2,1)S(1)}, u32[]{:S(2)}, u32[]{:S(2)}) collective-permute-start(bf16[2,4,96,128]{3,2,1,0:T(8,128)(2,1)S(1)} %slice.856), channel_id=1, source_target_pairs={{0,2},{2,4},{4,6},{6,8},{8,10},{10,12},{12,14},{1,3},{3,5},{5,7},{... | collective-permute-start | bytes 589832 | tf_op jit(solution)/shard_map/ppermute | solution.py:26
  25.4 4.9 %collective-permute-start.7 = (bf16[6,1,96,128]{3,2,1,0:T(8,128)(2,1)S(1)}, bf16[6,1,96,128]{3,2,1,0:T(8,128)(2,1)S(1)}, u32[]{:S(2)}, u32[]{:S(2)}) collective-permute-start(bf16[6,1,96,128]{3,2,1,0:T(8,128)(2,1)S(1)} %get-tuple-element.152), channel_id=1, source_target_pairs={{0,1},{2,3},{4,5},{6,7},{8,9},{10,11},{12,13},{14,15},{16,17},{18,... | collective-permute-start | bytes 442376 | tf_op jit(solution)/shard_map/ppermute | solution.py:17
  32.9 4.6 %collective-permute-start.1 = (bf16[6,1,96,128]{3,2,1,0:T(8,128)(2,1)S(1)}, bf16[6,1,96,128]{3,2,1,0:T(8,128)(2,1)S(1)}, u32[]{:S(2)}, u32[]{:S(2)}) collective-permute-start(bf16[6,1,96,128]{3,2,1,0:T(8,128)(2,1)S(1)} %get-tuple-element.161), channel_id=1, source_target_pairs={{0,1},{2,3},{4,5},{6,7},{8,9},{10,11},{12,13},{14,15},{16,17},{18,... | collective-permute-start | bytes 442376 | tf_op jit(solution)/shard_map/ppermute | solution.py:17
  39.9 2.0 fusion.211
  43.0 2.1 fusion.213
  63.6 3.0 %collective-permute-start.3 = (bf16[2,4,96,128]{3,2,1,0:T(8,128)(2,1)S(1)}, bf16[2,4,96,128]{3,2,1,0:T(8,128)(2,1)S(1)}, u32[]{:S(2)}, u32[]{:S(2)}) collective-permute-start(bf16[2,4,96,128]{3,2,1,0:T(8,128)(2,1)S(1)} %slice.896), channel_id=1, source_target_pairs={{0,2},{2,4},{4,6},{6,8},{8,10},{10,12},{12,14},{1,3},{3,5},{5,7},{... | collective-permute-start | bytes 589832 | tf_op jit(solution)/shard_map/ppermute | solution.py:26
  70.0 4.6 %collective-permute-start.4 = (bf16[6,1,96,128]{3,2,1,0:T(8,128)(2,1)S(1)}, bf16[6,1,96,128]{3,2,1,0:T(8,128)(2,1)S(1)}, u32[]{:S(2)}, u32[]{:S(2)}) collective-permute-start(bf16[6,1,96,128]{3,2,1,0:T(8,128)(2,1)S(1)} %get-tuple-element.157), channel_id=1, source_target_pairs={{0,1},{2,3},{4,5},{6,7},{8,9},{10,11},{12,13},{14,15},{16,17},{18,... | collective-permute-start | bytes 442376 | tf_op jit(solution)/shard_map/ppermute | solution.py:17
  74.6 1.3 collective-permute-start.10
  75.9 1.5 collective-permute-start.11
  79.0 2.3 collective-permute-done.10
  81.3 2.9 %collective-permute-done.11 = bf16[6,1,96,128]{3,2,1,0:T(8,128)(2,1)S(1)} collective-permute-done((bf16[6,1,96,128]{3,2,1,0:T(8,128)(2,1)S(1)}, bf16[6,1,96,128]{3,2,1,0:T(8,128)(2,1)S(1)}, u32[]{:S(2)}, u32[]{:S(2)}) %collective-permute-start.11) | collective-permute-done | bytes 147488 | tf_op jit(solution)/shard_map/ppermute | solution.py:18
  89.6 1.9 fusion.212
  98.9 1.3 convolution_add_fusion.19
  101.2 3.6 %fusion.210 = (bf16[4,4,96,128]{3,2,1,0:T(8,128)(2,1)}, bf16[4,4,96,128]{3,2,1,0:T(8,128)(2,1)}, bf16[4,4,96,128]{3,2,1,0:T(8,128)(2,1)}, bf16[4,4,96,128]{3,2,1...) fusion(bf16[6,6,96,130]{3,2,1,0:T(8,128)(2,1)S(1)} %select_maxi, ...), kind=kLoop, calls=%fused_computation.330 | loop fusion | bytes 14155776 | tf_op jit(solution)/shard_map/slice | solution.py:43
  105.2 1.8 fusion.78
  111.2 1.3 convolution_add_fusion.15
  116.2 1.4 fusion.12
  117.6 12.7 %reduce-scatter.5.cloned.1.call-done = f32[1296,96]{1,0:T(8,128)} async-done(((f32[2592,96]{1,0:T(8,128)}), f32[1296,96]{1,0:T(8,128)}) %reduce-scatter.5.cloned.1.call-update) | async-done | bytes 497680 | tf_op jit(solution)/shard_map/reduce_scatter | solution.py:124
  130.4 2.6 %fusion.16 = f32[1,4,4,96,128]{4,3,2,1,0:T(8,128)} fusion(f32[4,4,128,96]{2,3,1,0:T(8,128)} %convolution_add_fusion.15, bf16[288,96,1,1]{1,0,3,2:T(8,128)(2,1)S(1)} %bitcast.410, bf16[1,4,4,96,128]{4,3,2,1,0:T(8,128)(2,1)S(1)} %copy-done.1, bf16[4,4,96,128]{3,2,1,0:T(8,128)(2,1)S(1)} %get-tuple-element.65, ...), kind=kOutput, calls=%fused_computation.48 | convolution fusion | flops 117374976 | bytes 3201024 | tf_op jit(solution)/shard_map/frkw,kd->frdw/dot_general | solution.py:53
  136.2 42.6 %all-reduce.11.cloned.1.call-done = (f32[1296,96]{1,0:T(8,128)}, f32[1296,96]{1,0:T(8,128)}) async-done(((f32[1296,96]{1,0:T(8,128)}, f32[1296,96]{1,0:T(8,128)}), (f32[1296,96]{1,0:T(8,128)}, f32[1296,96]{1,0:T(8,128)})) %all-reduce.11.cloned.1.call-update) | async-done | bytes 995344 | tf_op jit(solution)/shard_map/psum | solution.py:121
  180.0 61.3 %all-reduce.9.cloned.1.call-done = (f32[1296,96]{1,0:T(8,128)}, f32[1296,96]{1,0:T(8,128)}) async-done(((f32[1296,96]{1,0:T(8,128)}, f32[1296,96]{1,0:T(8,128)}), (f32[1296,96]{1,0:T(8,128)}, f32[1296,96]{1,0:T(8,128)})) %all-reduce.9.cloned.1.call-update) | async-done | bytes 995344 | tf_op jit(solution)/shard_map/psum | solution.py:121
  241.3 2.1 copy.104
  243.4 2.1 copy.105
  (293 shorter events, 68.0 us)
Async XLA Ops:
  7.2 8.6 %copy-start.20 = (bf16[2592,96]{0,1:T(8,128)(2,1)S(1)}, bf16[2592,96]{0,1:T(8,128)(2,1)}, u32[]{:S(2)}) copy-start(bf16[2592,96]{0,1:T(8,128)(2,1)} %param.6) | copy-start | bytes 1492996
  7.2 110.4 %reduce-scatter.3.cloned.1.call-start = ((), (), s32[]{:S(2)}) async-start(), calls=%async_computation.2 | async-start | bytes 1990656 | tf_op jit(solution)/shard_map/reduce_scatter | solution.py:123
  8.9 16.5 %collective-permute-start.6 = (bf16[2,4,96,128]{3,2,1,0:T(8,128)(2,1)}, bf16[2,4,96,128]{3,2,1,0:T(8,128)(2,1)S(1)}, u32[]{:S(2)}, u32[]{:S(2)}) collective-permute-start(bf16[2,4,96,128]{3,2,1,0:T(8,128)(2,1)} %slice_bitcast_fusion), channel_id=1, source_target_pairs={{2,0},{4,2},{6,4},{8,6},{10,8},{12,10},{14,12},{3,1},{5,3},{7,5},{... | collective-permute-start | bytes 589832 | tf_op jit(solution)/shard_map/ppermute | solution.py:26
  12.5 4.4 %copy-start.21 = (bf16[2592,96]{0,1:T(8,128)(2,1)S(1)}, bf16[2592,96]{0,1:T(8,128)(2,1)}, u32[]{:S(2)}) copy-start(bf16[2592,96]{0,1:T(8,128)(2,1)} %param.7) | copy-start | bytes 1492996
  12.5 19.0 %collective-permute-start = (bf16[2,4,96,128]{3,2,1,0:T(8,128)(2,1)S(1)}, bf16[2,4,96,128]{3,2,1,0:T(8,128)(2,1)S(1)}, u32[]{:S(2)}, u32[]{:S(2)}) collective-permute-start(bf16[2,4,96,128]{3,2,1,0:T(8,128)(2,1)S(1)} %slice.856), channel_id=1, source_target_pairs={{0,2},{2,4},{4,6},{6,8},{8,10},{10,12},{12,14},{1,3},{3,5},{5,7},{... | collective-permute-start | bytes 589832 | tf_op jit(solution)/shard_map/ppermute | solution.py:26
  18.2 7.1 %copy-start = (bf16[1,4,4,96,128]{4,3,2,1,0:T(8,128)(2,1)S(1)}, bf16[1,4,4,96,128]{4,3,2,1,0:T(8,128)(2,1)}, u32[]{:S(2)}) copy-start(bf16[1,4,4,96,128]{4,3,2,1,0:T(8,128)(2,1)} %param.5) | copy-start | bytes 1179652
  25.4 12.2 %collective-permute-start.7 = (bf16[6,1,96,128]{3,2,1,0:T(8,128)(2,1)S(1)}, bf16[6,1,96,128]{3,2,1,0:T(8,128)(2,1)S(1)}, u32[]{:S(2)}, u32[]{:S(2)}) collective-permute-start(bf16[6,1,96,128]{3,2,1,0:T(8,128)(2,1)S(1)} %get-tuple-element.152), channel_id=1, source_target_pairs={{0,1},{2,3},{4,5},{6,7},{8,9},{10,11},{12,13},{14,15},{16,17},{18,... | collective-permute-start | bytes 442376 | tf_op jit(solution)/shard_map/ppermute | solution.py:17
  30.3 8.6 %collective-permute-start.8 = (bf16[6,1,96,128]{3,2,1,0:T(8,128)(2,1)S(1)}, bf16[6,1,96,128]{3,2,1,0:T(8,128)(2,1)S(1)}, u32[]{:S(2)}, u32[]{:S(2)}) collective-permute-start(bf16[6,1,96,128]{3,2,1,0:T(8,128)(2,1)S(1)} %get-tuple-element.153), channel_id=1, source_target_pairs={{1,0},{3,2},{5,4},{7,6},{9,8},{11,10},{13,12},{15,14},{17,16},{19,... | collective-permute-start | bytes 442376 | tf_op jit(solution)/shard_map/ppermute | solution.py:18
  31.6 10.4 %collective-permute-start.2 = (bf16[6,1,96,128]{3,2,1,0:T(8,128)(2,1)S(1)}, bf16[6,1,96,128]{3,2,1,0:T(8,128)(2,1)S(1)}, u32[]{:S(2)}, u32[]{:S(2)}) collective-permute-start(bf16[6,1,96,128]{3,2,1,0:T(8,128)(2,1)S(1)} %get-tuple-element.160), channel_id=1, source_target_pairs={{1,0},{3,2},{5,4},{7,6},{9,8},{11,10},{13,12},{15,14},{17,16},{19,... | collective-permute-start | bytes 442376 | tf_op jit(solution)/shard_map/ppermute | solution.py:18
  32.9 9.1 %collective-permute-start.1 = (bf16[6,1,96,128]{3,2,1,0:T(8,128)(2,1)S(1)}, bf16[6,1,96,128]{3,2,1,0:T(8,128)(2,1)S(1)}, u32[]{:S(2)}, u32[]{:S(2)}) collective-permute-start(bf16[6,1,96,128]{3,2,1,0:T(8,128)(2,1)S(1)} %get-tuple-element.161), channel_id=1, source_target_pairs={{0,1},{2,3},{4,5},{6,7},{8,9},{10,11},{12,13},{14,15},{16,17},{18,... | collective-permute-start | bytes 442376 | tf_op jit(solution)/shard_map/ppermute | solution.py:17
  62.3 12.2 %collective-permute-start.9 = (bf16[2,4,96,128]{3,2,1,0:T(8,128)(2,1)S(1)}, bf16[2,4,96,128]{3,2,1,0:T(8,128)(2,1)S(1)}, u32[]{:S(2)}, u32[]{:S(2)}) collective-permute-start(bf16[2,4,96,128]{3,2,1,0:T(8,128)(2,1)S(1)} %slice.975), channel_id=1, source_target_pairs={{2,0},{4,2},{6,4},{8,6},{10,8},{12,10},{14,12},{3,1},{5,3},{7,5},{... | collective-permute-start | bytes 589832 | tf_op jit(solution)/shard_map/ppermute | solution.py:26
  63.6 5.0 %collective-permute-start.3 = (bf16[2,4,96,128]{3,2,1,0:T(8,128)(2,1)S(1)}, bf16[2,4,96,128]{3,2,1,0:T(8,128)(2,1)S(1)}, u32[]{:S(2)}, u32[]{:S(2)}) collective-permute-start(bf16[2,4,96,128]{3,2,1,0:T(8,128)(2,1)S(1)} %slice.896), channel_id=1, source_target_pairs={{0,2},{2,4},{4,6},{6,8},{8,10},{10,12},{12,14},{1,3},{3,5},{5,7},{... | collective-permute-start | bytes 589832 | tf_op jit(solution)/shard_map/ppermute | solution.py:26
  68.6 61.7 %reduce-scatter.5.cloned.1.call-start = ((), (), s32[]{:S(2)}) async-start(), calls=%async_computation.3 | async-start | bytes 1990656 | tf_op jit(solution)/shard_map/reduce_scatter | solution.py:124
  68.7 17.8 %collective-permute-start.5 = (bf16[6,1,96,128]{3,2,1,0:T(8,128)(2,1)S(1)}, bf16[6,1,96,128]{3,2,1,0:T(8,128)(2,1)S(1)}, u32[]{:S(2)}, u32[]{:S(2)}) collective-permute-start(bf16[6,1,96,128]{3,2,1,0:T(8,128)(2,1)S(1)} %get-tuple-element.156), channel_id=1, source_target_pairs={{1,0},{3,2},{5,4},{7,6},{9,8},{11,10},{13,12},{15,14},{17,16},{19,... | collective-permute-start | bytes 442376 | tf_op jit(solution)/shard_map/ppermute | solution.py:18
  70.0 16.5 %collective-permute-start.4 = (bf16[6,1,96,128]{3,2,1,0:T(8,128)(2,1)S(1)}, bf16[6,1,96,128]{3,2,1,0:T(8,128)(2,1)S(1)}, u32[]{:S(2)}, u32[]{:S(2)}) collective-permute-start(bf16[6,1,96,128]{3,2,1,0:T(8,128)(2,1)S(1)} %get-tuple-element.157), channel_id=1, source_target_pairs={{0,1},{2,3},{4,5},{6,7},{8,9},{10,11},{12,13},{14,15},{16,17},{18,... | collective-permute-start | bytes 442376 | tf_op jit(solution)/shard_map/ppermute | solution.py:17
  74.6 6.7 %collective-permute-start.10 = (bf16[6,1,96,128]{3,2,1,0:T(8,128)(2,1)S(1)}, bf16[6,1,96,128]{3,2,1,0:T(8,128)(2,1)S(1)}, u32[]{:S(2)}, u32[]{:S(2)}) collective-permute-start(bf16[6,1,96,128]{3,2,1,0:T(8,128)(2,1)S(1)} %get-tuple-element.148), channel_id=1, source_target_pairs={{0,1},{2,3},{4,5},{6,7},{8,9},{10,11},{12,13},{14,15},{16,17},{18,... | collective-permute-start | bytes 442376 | tf_op jit(solution)/shard_map/ppermute | solution.py:17
  75.9 8.3 %collective-permute-start.11 = (bf16[6,1,96,128]{3,2,1,0:T(8,128)(2,1)S(1)}, bf16[6,1,96,128]{3,2,1,0:T(8,128)(2,1)S(1)}, u32[]{:S(2)}, u32[]{:S(2)}) collective-permute-start(bf16[6,1,96,128]{3,2,1,0:T(8,128)(2,1)S(1)} %get-tuple-element.149), channel_id=1, source_target_pairs={{1,0},{3,2},{5,4},{7,6},{9,8},{11,10},{13,12},{15,14},{17,16},{19,... | collective-permute-start | bytes 442376 | tf_op jit(solution)/shard_map/ppermute | solution.py:18
  101.2 4.0 %copy-start.51 = (bf16[3,1,1,96,96]{4,3,0,2,1:T(8,128)(2,1)S(1)}, bf16[3,1,1,96,96]{4,3,0,2,1:T(8,128)(2,1)}, u32[]{:S(2)}) copy-start(bf16[3,1,1,96,96]{4,3,0,2,1:T(8,128)(2,1)} %copy.77) | copy-start | bytes 165892
  104.9 74.0 %all-reduce.11.cloned.1.call-start = ((), (), s32[]{:S(2)}) async-start(), calls=%async_computation.5 | async-start | bytes 2654208 | tf_op jit(solution)/shard_map/psum | solution.py:121
  116.2 14.2 %copy-start.1 = (bf16[1,4,4,96,128]{4,3,2,1,0:T(8,128)(2,1)S(1)}, bf16[1,4,4,96,128]{4,3,2,1,0:T(8,128)(2,1)}, u32[]{:S(2)}) copy-start(bf16[1,4,4,96,128]{4,3,2,1,0:T(8,128)(2,1)} %param.4) | copy-start | bytes 1179652
  116.2 14.2 %copy-start.52 = (bf16[3,1,1,96,96]{4,3,2,1,0:T(8,128)(2,1)S(1)}, bf16[3,1,1,96,96]{4,3,2,1,0:T(8,128)(2,1)}, u32[]{:S(2)}) copy-start(bf16[3,1,1,96,96]{4,3,2,1,0:T(8,128)(2,1)} %get-tuple-element.128) | copy-start | bytes 165892
  130.3 111.0 %all-reduce.9.cloned.1.call-start = ((), (), s32[]{:S(2)}) async-start(), calls=%async_computation.4 | async-start | bytes 2654208 | tf_op jit(solution)/shard_map/psum | solution.py:121
  130.4 2.7 %copy-start.25 = (bf16[4,4,96,128]{3,2,1,0:T(8,128)(2,1)S(1)}, bf16[4,4,96,128]{3,2,1,0:T(8,128)(2,1)}, u32[]{:S(2)}) copy-start(bf16[4,4,96,128]{3,2,1,0:T(8,128)(2,1)} %get-tuple-element.14) | copy-start | bytes 1179652
  130.4 2.7 %copy-start.26 = (bf16[4,4,96,128]{3,2,1,0:T(8,128)(2,1)S(1)}, bf16[4,4,96,128]{3,2,1,0:T(8,128)(2,1)}, u32[]{:S(2)}) copy-start(bf16[4,4,96,128]{3,2,1,0:T(8,128)(2,1)} %get-tuple-element.15) | copy-start | bytes 1179652
  (63 other events, 76.4 us)
Sparse Core Ops, SparseCore 0:
  68.7 24.6 reduce-scatter.2
  105.0 25.2 reduce-scatter.4
  132.6 46.1 all-reduce.10
  181.1 60.0 all-reduce.8
